TPU v7x, 128 devices: a whole 4x4x4 slice. The times are simulated.
128 devices in a mesh: inp: 16 (over y, x_lo, core), spec: 8 (over x_hi, z).
Axes of the slice: x: 4 (x_hi: 2, x_lo: 2; x = x_hi * 2 + x_lo), y: 4, z: 4, core: 2. Of those that a mesh axis runs over, the one named last changes fastest.
Arguments:
- voltages: bfloat16 [2048, 262144], P('inp', 'spec'), may hold values from -6 to 6
Outputs:
- visibilities: float32 [128, 136, 2, 128, 128], P(('inp', 'spec'))
All inputs are finite; a program needn't handle non-finite values.
Results may differ from a plain program's by a relative error of at most 0.0054.
Values may be sent and summed in bfloat16 or wider, within the bound.
A program may use at most 128 MiB of HBM per device.

v0:
```python
import math

import jax
import jax.numpy as jnp
import numpy as np
from jax import lax
from jax.sharding import PartitionSpec as P

NFFT = 2048
NTAP = 4
TB = 128
CH_DEV = 1


def shifted(value, axis, steps):
    count = lax.axis_size(axis)
    initial, last = (max(0, -steps), min(count, count - steps))
    return lax.ppermute(value, axis, [(source, source + steps) for source in range(initial, last)])


def in_blocks(array, dim, size):
    before, after = (array.shape[:dim], array.shape[dim + 1 :])
    return jnp.moveaxis(array.reshape(*before, size, -1, *after), dim, 0)


def laid_out(pieces, dim):
    dims = list(pieces.shape[1:])
    dims[dim] *= pieces.shape[0]
    return jnp.moveaxis(pieces, 0, dim).reshape(dims)


def one_exchange(array, axis, axes, splits, concats):
    sizes = [lax.axis_size(a) for a in axes]
    pieces = in_blocks(array, splits[0], sizes[0])
    pieces = jnp.moveaxis(in_blocks(pieces, splits[1] + 1, sizes[1]), 0, 1)
    inside = pieces.shape[2:]
    pieces = pieces.reshape(-1, *inside)
    pieces = lax.all_to_all(pieces, axis, split_axis=0, concat_axis=0, tiled=True)
    pieces = laid_out(pieces.reshape(*sizes, *inside), concats[0] + 1)
    return laid_out(pieces, concats[1])


def window_taps(ntaps, nfft):
    sample_pos = jnp.arange(ntaps * nfft, dtype=jnp.float32)
    centered = (sample_pos - 0.5 * ntaps * nfft) / nfft
    hann_part = 0.5 - 0.5 * jnp.cos(sample_pos * (2.0 * math.pi / (ntaps * nfft)))
    return (jnp.sinc(centered) * hann_part).reshape(ntaps, nfft)


def dft_columns(nfft, chan_total, chan_step):
    sample_idx = jnp.arange(nfft, dtype=jnp.int32)
    chan_freq = jnp.arange(chan_total, dtype=jnp.int32) * chan_step + chan_step // 2
    phase_int = sample_idx[:, None] * chan_freq[None, :] % nfft
    phase_angle = phase_int.astype(jnp.float32) * (2.0 * math.pi / nfft)
    dft_norm = 1.0 / math.sqrt(nfft)
    stacked = jnp.stack([jnp.cos(phase_angle) * dft_norm, -jnp.sin(phase_angle) * dft_norm], axis=2)
    return stacked.reshape(nfft, 2 * chan_total)


def filter_kernel(ntaps, nfft, chan_total, chan_step):
    taps = window_taps(ntaps, nfft)
    columns = dft_columns(nfft, chan_total, chan_step)
    return (taps[:, :, None] * columns[None, :, :]).astype(jnp.bfloat16)


def tap_products(frames, kernel):
    return jnp.einsum("ifn,tnq->tqfi", frames, kernel, preferred_element_type=jnp.float32)


def tap_sum(products, count):
    total = products[0, :, 0:count]
    for tap_index in range(1, products.shape[0]):
        total = total + products[tap_index, :, tap_index : tap_index + count]
    return total


def correlate_block(chan_block):
    chan_count, pair_dim, spec_total, input_count = chan_block.shape
    stacked_rows = chan_block.reshape(chan_count, 2 * spec_total, input_count)
    turned = jnp.concatenate([-chan_block[:, 1], chan_block[:, 0]], axis=1)
    inv_count = 1.0 / spec_total
    row_blocks = input_count // TB
    real_part = jnp.einsum(
        "cri,crj->cij", stacked_rows, stacked_rows, preferred_element_type=jnp.float32
    )
    imag_part = jnp.einsum("cri,crj->cij", stacked_rows, turned, preferred_element_type=jnp.float32)
    pair_parts = jnp.stack([real_part, imag_part], axis=1) * inv_count
    tiled = pair_parts.reshape(chan_count, 2, row_blocks, TB, row_blocks, TB).transpose(
        0, 2, 4, 1, 3, 5
    )
    row_index, col_index = np.triu_indices(row_blocks)
    return tiled[:, row_index, col_index]


def shards(voltages):
    local_inputs, samples = voltages.shape
    local_spectra = samples // NFFT
    inp_count = lax.axis_size("inp")
    spec_count = lax.axis_size("spec")
    chan_total = CH_DEV * inp_count * spec_count
    chan_step = NFFT // 2 // chan_total
    kernel = filter_kernel(NTAP, NFFT, chan_total, chan_step)
    lead = NTAP - 1
    own_frames = voltages.reshape(local_inputs, local_spectra, NFFT)
    products = tap_products(own_frames, kernel)
    front = jnp.pad(products, ((0, 0), (0, 0), (lead, 0), (0, 0)))
    spectra = tap_sum(front, local_spectra)
    tail = jnp.pad(products[:, :, local_spectra - lead :], ((0, 0), (0, 0), (0, lead), (0, 0)))
    outgoing = tap_sum(tail, lead)
    arrived_terms = shifted(outgoing, "spec", 1)
    spectra = jnp.concatenate([spectra[:, :lead] + arrived_terms, spectra[:, lead:]], axis=1)
    spectra = spectra.astype(jnp.bfloat16)
    send_block = spectra.reshape(inp_count, spec_count, CH_DEV, 2, local_spectra, local_inputs)
    arrived = one_exchange(send_block, ("inp", "spec"), ("inp", "spec"), (0, 1), (5, 4))
    arranged = arrived.reshape(CH_DEV, 2, spec_count * local_spectra, inp_count * local_inputs)
    return correlate_block(arranged)


def solution(mesh):
    return jax.shard_map(
        shards,
        mesh=mesh,
        in_specs=(P("inp", "spec"),),
        out_specs=P(("inp", "spec"), None, None, None, None),
        check_vma=False,
    )
```

profile of v0, /device:TPU:1, one launch (start us, length us, event | category | flops | bytes accessed | tf_op | source)
XLA Modules:
  0.0 102.3 jit_solution(10417261256749073851)
XLA Ops:
  0.0 0.3 fusion.30
  0.3 4.2 %cosine_multiply_fusion = (f32[2048,128,1]{1,0,2:T(8,128)S(1)}, f32[2048,128,1]{1,0,2:T(8,128)S(1)}) fusion(s32[128]{0:T(128)S(1)} %multiply_add_fusion.1), kind=kLoop, calls=%fused_computation.34 | loop fusion | flops 4456448 | bytes 2097664 | tf_op jit(solution)/shard_map/mul | solution.py:56
  4.5 0.1 pad_maximum_fusion
  4.6 2.3 %copy.37 = f32[2048,128,2]{0,2,1:T(2,128)} copy(f32[2048,128,2]{1,0,2:T(8,128)S(1)} %pad_maximum_fusion) | data formatting | bytes 4194304 | tf_op jit(solution)/shard_map/stack | solution.py:56
  7.0 2.7 %mul.254 = f32[2048,256]{0,1:T(8,128)S(1)} reshape(f32[2048,128,2]{0,2,1:T(2,128)} %copy.37) | data formatting | bytes 4194304 | tf_op jit(solution)/shard_map/mul | solution.py:63
  9.7 11.3 %fusion.7 = f32[4,256,16,128]{3,1,2,0:T(8,128)S(1)} fusion(bf16[16,16,8,2048]{3,2,1,0:T(8,128)(2,1)} %bitcast.81, f32[2048,256]{0,1:T(8,128)S(1)} %mul.254, f32[4,2048]{1,0:T(4,128)S(1)} %fusion.30), kind=kOutput, calls=%fused_computation.17 | convolution fusion | flops 8594128896 | bytes 18907136 | tf_op jit(solution)/shard_map/ifn,tnq->tqfi/dot_general | solution.py:67
  21.0 0.1 slice.58
  21.1 4.6 %collective-permute-start = (f32[256,3,128]{2,0,1:T(8,128)S(1)}, f32[256,3,128]{2,0,1:T(8,128)S(1)}, u32[]{:S(2)}, u32[]{:S(2)}) collective-permute-start(f32[256,3,128]{2,0,1:T(8,128)S(1)} %fusion.23), channel_id=1, source_target_pairs={{0,1},{1,2},{2,3},{3,4},{4,5},{5,6},{6,7},{8,9},{9,10},{10,11},{11... | collective-permute-start | bytes 1179656 | tf_op jit(solution)/shard_map/ppermute | solution.py:18
  25.7 0.5 fusion.13
  26.2 0.1 slice.97
  26.4 1.0 copy.40
  27.4 5.9 %collective-permute-done = f32[256,3,128]{2,0,1:T(8,128)S(1)} collective-permute-done((f32[256,3,128]{2,0,1:T(8,128)S(1)}, f32[256,3,128]{2,0,1:T(8,128)S(1)}, u32[]{:S(2)}, u32[]{:S(2)}) %collective-permute-start) | collective-permute-done | bytes 393248 | tf_op jit(solution)/shard_map/ppermute | solution.py:18
  33.3 0.3 copy.39
  33.6 0.5 pad_maximum_fusion.1
  34.1 30.4 %all_to_all.5 = bf16[128,1,1,1,2,16,128]{6,5,4,3,2,1,0:T(8,128)(2,1)S(1)} all-to-all(bf16[128,1,1,1,2,16,128]{6,5,4,3,2,1,0:T(8,128)(2,1)S(1)} %pad_maximum_fusion.1), channel_id=1, replica_groups=mesh['inp'=16,'spec'=8] {'inp','spec'}, dimensions={0} | all-to-all | bytes 2097152 | tf_op jit(solution)/shard_map/all_to_all | solution.py:38
  64.5 0.3 copy.57
  64.8 0.1 copy.42
  64.9 0.5 copy.43
  65.5 1.1 %maximum_bitcast_fusion = bf16[2048,256]{0,1:T(8,128)(2,1)} fusion(bf16[1,128,2048]{2,1,0:T(8,128)(2,1)S(1)} %get-tuple-element.6, bf16[1,128,2048]{2,1,0:T(8,128)(2,1)S(1)} %get-tuple-element.5), kind=kLoop, calls=%fused_computation.32 | loop fusion | flops 2097152 | bytes 2097152 | tf_op jit(solution)/shard_map/cri,crj->cij/dot_general | solution.py:86
  66.6 1.5 %copy.45 = bf16[2048,256]{1,0:T(8,128)(2,1)S(1)} copy(bf16[2048,256]{0,1:T(8,128)(2,1)} %maximum_bitcast_fusion) | data formatting | bytes 2097152 | tf_op jit(solution)/shard_map/cri,crj->cij/dot_general | solution.py:86
  68.0 2.4 %convolution_bitcast_fusion = f32[1,1,16,128,16,128]{5,3,4,2,1,0:T(8,128)S(1)} fusion(bf16[16,128,256,1]{2,1,3,0:T(8,128)(2,1)S(1)} %bitcast.71, bf16[16,128,256,1]{2,1,0,3:T(8,128)(2,1)S(1)} %bitcast.76), kind=kOutput, calls=%fused_computation.6 | convolution fusion | flops 2147483648 | bytes 18874368 | tf_op jit(solution)/shard_map/cri,crj->cij/dot_general | solution.py:86
  70.4 2.4 %convolution_bitcast_fusion.1 = f32[1,1,16,128,16,128]{5,3,4,2,1,0:T(8,128)S(1)} fusion(bf16[16,128,256,1]{2,1,3,0:T(8,128)(2,1)S(1)} %bitcast.72, bf16[16,128,256,1]{2,1,0,3:T(8,128)(2,1)S(1)} %bitcast.73), kind=kOutput, calls=%fused_computation.7 | convolution fusion | flops 2147483648 | bytes 18874368 | tf_op jit(solution)/shard_map/cri,crj->cij/dot_general | solution.py:83
  72.8 11.7 %fusion = f32[16,16,2,128,128]{4,3,1,0,2:T(8,128)} fusion(f32[1,1,16,128,16,128]{5,3,4,2,1,0:T(8,128)S(1)} %convolution_bitcast_fusion, f32[1,1,16,128,16,128]{5,3,4,2,1,0:T(8,128)S(1)} %convolution_bitcast_fusion.1), kind=kLoop, calls=%fused_computation.2 | loop fusion | flops 16777216 | bytes 67108864 | tf_op jit(solution)/shard_map/transpose | solution.py:88
  84.6 17.6 %gather_fusion = f32[136,2,128,128]{3,2,1,0:T(8,128)} fusion(f32[16,16,2,128,128]{4,3,1,0,2:T(8,128)} %fusion, s32[136]{0:T(256)S(1)} %copy-done), kind=kCustom, calls=%fused_computation | custom fusion | bytes 35652672 | tf_op jit(solution)/shard_map/gather | solution.py:92
  (6 shorter events, 0.2 us)
Async XLA Ops:
  21.1 12.1 %collective-permute-start = (f32[256,3,128]{2,0,1:T(8,128)S(1)}, f32[256,3,128]{2,0,1:T(8,128)S(1)}, u32[]{:S(2)}, u32[]{:S(2)}) collective-permute-start(f32[256,3,128]{2,0,1:T(8,128)S(1)} %fusion.23), channel_id=1, source_target_pairs={{0,1},{1,2},{2,3},{3,4},{4,5},{5,6},{6,7},{8,9},{9,10},{10,11},{11... | collective-permute-start | bytes 1179656 | tf_op jit(solution)/shard_map/ppermute | solution.py:18
  72.8 11.7 %copy-start = (s32[136]{0:T(256)S(1)}, s32[136]{0:T(256)}, u32[]{:S(2)}) copy-start(s32[136]{0:T(256)} %constant.115) | copy-start | bytes 1636
where the time goes:
time: 103 us; the launch traced here: 102 us
  blocking collectives  30.4 us (30%)
  local copies, waits for them, and re-layouts  26.6 us (26%)
  other arithmetic  18.6 us (18%)
  matrix products  16.1 us (16%)
  waiting for transfers between devices  5.88 us (6%)
  starting transfers between devices  4.57 us (4%)
    all_to_all x1, blocking collectives, one_exchange(): lax.all_to_all(pieces, axis, split_axis=0, concat_axis=0, tiled=True)  30.4 us
    gather x1, local copies, waits for them, and re-layouts, correlate_block(): return tiled[:, row_index, col_index]  17.6 us
    transpose x1, other arithmetic, correlate_block(): pair_parts.reshape(chan_count, 2, row_blocks, TB, row_blocks, TB)  11.7 us
    dot_general x1, matrix products, tap_products(): jnp.einsum('ifn,tnq->tqfi', frames, kernel, preferred_element_type=jnp.fl...  11.3 us
    ppermute x1, waiting for transfers between devices, shifted(): lax.ppermute(value, axis, [(source, source + steps) for source in range(i...  5.88 us
    ppermute x1, starting transfers between devices, shifted(): lax.ppermute(value, axis, [(source, source + steps) for source in range(i...  4.57 us
    mul x1, other arithmetic, dft_columns(): jnp.cos(phase_angle) * dft_norm  4.17 us
    mul x1, local copies, waits for them, and re-layouts, filter_kernel(): return (taps[:, :, None] * columns[None, :, :]).astype(jnp.bfloat16)  2.69 us
  transfers between devices with their start and end apart: 1, of which 1 were waited for; matrix products, arithmetic and copies ran while one was open for 2% of the time, Pallas kernels for 0%

commit v1 on v0

v1 whole, which is shorter than its diff:
```python
import functools
import math

import jax
import jax.numpy as jnp
import numpy as np
import ml_dtypes
from jax import lax
from jax.experimental import pallas as pl
from jax.experimental.pallas import tpu as pltpu
from jax.sharding import PartitionSpec as P

NFFT = 2048
NTAP = 4
TB = 128
CHANS = 128
STEP = 8
FRAMES = 16
CHUNKS = 4
PER = CHANS // CHUNKS
ROWS = 2 * PER
LOGICAL = pl.DeviceIdType.LOGICAL


def filter_rows():
    pos = np.arange(NTAP * NFFT, dtype=np.float64)
    window = np.sinc((pos - 0.5 * NTAP * NFFT) / NFFT) * (0.5 - 0.5 * np.cos(2.0 * math.pi * pos / (NTAP * NFFT)))
    freq = np.arange(CHANS) * STEP + STEP // 2
    angle = (np.arange(NFFT)[:, None] * freq[None, :] % NFFT) * (2.0 * math.pi / NFFT)
    columns = np.stack([np.cos(angle), -np.sin(angle)], axis=2) / math.sqrt(NFFT)
    window = window.astype(np.float32).reshape(NTAP, NFFT, 1)
    columns = columns.astype(np.float32).reshape(1, NFFT, 2 * CHANS)
    kernel = (window * columns).astype(ml_dtypes.bfloat16)
    kernel = kernel.transpose(0, 2, 1).reshape(NTAP, CHUNKS, ROWS, NFFT)
    return np.ascontiguousarray(kernel.transpose(1, 0, 2, 3)).reshape(CHUNKS, NTAP * ROWS, NFFT)


def far_first():
    hops = lambda d: min(d, 4 - d)
    all_of = [(dx, dz, dc) for dx in range(4) for dz in range(4) for dc in range(2)]
    return sorted(all_of, key=lambda o: (-hops(o[0]) - hops(o[1]), -o[2], (o[0] * 7 + o[1] * 5) % 11))


def spread_kernel(v_ref, k_ref, r_ref, vbuf, kbuf, prod, acc, tail, out, vsem, ksem, ssem, rsem, lsem):
    a, b = lax.axis_index("inp"), lax.axis_index("spec")
    me = a * 8 + b
    y, x_lo, core = lax.div(a, 4), lax.rem(lax.div(a, 2), 2), lax.rem(a, 2)
    x, z = lax.div(b, 4) * 2 + x_lo, lax.rem(b, 4)

    def plane(c):
        return lax.rem(y + 2 + c - lax.div(c, 2) * (2 * c - 1), 4)

    def k_copy(c):
        return pltpu.make_async_copy(k_ref.at[plane(c)], kbuf.at[c], ksem.at[c])

    def v_copy(f):
        return pltpu.make_async_copy(v_ref.at[:, pl.ds(pl.multiple_of(f * NFFT, NFFT), NFFT)], vbuf.at[f], vsem.at[f])

    k_copy(0).start()
    for f in range(FRAMES):
        v_copy(f).start()
    for c in range(1, CHUNKS):
        k_copy(c).start()

    barrier = pltpu.get_barrier_semaphore()

    def greet(k, carry):
        pl.semaphore_signal(barrier, inc=1, device_id=lax.rem(me + k, 128), device_id_type=LOGICAL)
        return carry

    lax.fori_loop(1, 128, greet, 0)
    tail[...] = jnp.zeros_like(tail)

    def chunk(c, carry):
        k_copy(c).wait()

        def pair(g, carry):
            @pl.when(c == 0)
            def _():
                v_copy(2 * g).wait()
                v_copy(2 * g + 1).wait()

            frames = vbuf[pl.ds(2 * g, 2)].reshape(2 * 128, NFFT)
            got = lax.dot_general(kbuf[c], frames, (((1,), (1,)), ((), ())), preferred_element_type=jnp.float32)
            prod[2 * g] = got[:, :128]
            prod[2 * g + 1] = got[:, 128:]
            return carry

        lax.fori_loop(0, FRAMES // 2, pair, 0)

        def group(g, carry):
            for s in range(FRAMES + NTAP - 1):
                total = None
                for t in range(NTAP):
                    f = s + t - (NTAP - 1)
                    if 0 <= f < FRAMES:
                        term = prod[f, pl.ds(pl.multiple_of(t * ROWS + 8 * g, 8), 8), :]
                        total = term if total is None else total + term
                if s < FRAMES:
                    acc[pl.ds(8 * g * FRAMES + s, 8, stride=FRAMES), :] = total
                else:
                    tail[pl.ds(8 * g * 4 + s - FRAMES, 8, stride=4), :] = total
            return carry

        lax.fori_loop(0, ROWS // 8, group, 0)

        def pack(l, carry):
            for k in range(4):
                out[c, l, k] = acc[pl.ds(pl.multiple_of(l * 32 + k * 8, 8), 8), :].astype(jnp.bfloat16)
            out[c, l, 4] = tail[pl.ds(pl.multiple_of(l * 8, 8), 8), :].astype(jnp.bfloat16)
            return carry

        lax.fori_loop(0, PER, pack, 0)

        @pl.when(c == 0)
        def _():
            pl.semaphore_wait(barrier, 127)

        y_to = plane(c)

        def send(dx, dz, dc):
            x_to, z_to = lax.rem(x + dx, 4), lax.rem(z + dz, 4)
            l = (lax.rem(x_to, 2) * 2 + lax.rem(core + dc, 2)) * 8 + lax.div(x_to, 2) * 4 + z_to
            pltpu.make_async_remote_copy(
                src_ref=out.at[c, l],
                dst_ref=r_ref.at[me],
                send_sem=ssem,
                recv_sem=rsem,
                device_id=y_to * 32 + l,
                device_id_type=LOGICAL,
            ).start()

        for offset in far_first()[:-1]:
            send(*offset)

        @pl.when(c < CHUNKS - 1)
        def _():
            send(0, 0, 0)

        return carry

    lax.fori_loop(0, CHUNKS, chunk, 0)
    own = pltpu.make_async_copy(out.at[CHUNKS - 1, lax.rem(me, 32)], r_ref.at[me], lsem)
    own.start()
    own.wait()
    landed = r_ref.at[pl.ds(0, 127)]
    pltpu.make_async_copy(landed, landed, ssem).wait()
    pltpu.make_async_copy(landed, landed, rsem).wait()


def spread(v, kernel):
    return pl.pallas_call(
        spread_kernel,
        out_shape=jax.ShapeDtypeStruct((128, 5, 8, 128), jnp.bfloat16),
        in_specs=[pl.BlockSpec(memory_space=pl.ANY)] * 2,
        out_specs=pl.BlockSpec(memory_space=pltpu.VMEM),
        scratch_shapes=[
            pltpu.VMEM((FRAMES, 128, NFFT), jnp.bfloat16),
            pltpu.VMEM((CHUNKS, NTAP * ROWS, NFFT), jnp.bfloat16),
            pltpu.VMEM((FRAMES, NTAP * ROWS, 128), jnp.float32),
            pltpu.VMEM((ROWS * FRAMES, 128), jnp.float32),
            pltpu.VMEM((ROWS * 4, 128), jnp.float32),
            pltpu.VMEM((CHUNKS, PER, 5, 8, 128), jnp.bfloat16),
            pltpu.SemaphoreType.DMA((FRAMES,)),
            pltpu.SemaphoreType.DMA((CHUNKS,)),
            pltpu.SemaphoreType.DMA,
            pltpu.SemaphoreType.DMA,
            pltpu.SemaphoreType.DMA,
        ],
        compiler_params=pltpu.CompilerParams(collective_id=0, has_side_effects=True, vmem_limit_bytes=40 << 20),
        name="spread",
    )(v, kernel)


BLOCKS = 16
TILES = BLOCKS * (BLOCKS + 1) // 2


def tile_index(r, c):
    return r * BLOCKS - r * (r - 1) // 2 + (c - r)


def correlate_kernel(r_ref, o_ref, left, right, stage, sem):
    row = lax.broadcasted_iota(jnp.int32, (8, 128), 0)
    for c in range(BLOCKS):
        for part in range(2):
            for b in range(8):
                src = c * 8 + b
                head = r_ref[src, 2 * part].astype(jnp.float32)
                rest = r_ref[src, 2 * part + 1].astype(jnp.float32)
                if b > 0:
                    terms = r_ref[src - 1, 4].astype(jnp.float32)
                    if part == 1:
                        terms = jnp.concatenate([terms[4:], terms[:4]], axis=0)
                    head = head + jnp.where(row < NTAP - 1, terms, 0.0)
                both = jnp.concatenate([head, rest], axis=0)
                at = part * 128 + b * 16
                right[c % 2, pl.ds(at, 16), 0:128] = both.astype(jnp.bfloat16)
        re, im = right[c % 2, 0:128, 0:128], right[c % 2, 128:256, 0:128]
        right[c % 2, 0:128, 128:256] = -im
        right[c % 2, 128:256, 128:256] = re
        left[c * 128 : (c + 1) * 128, 0:128] = re.T
        left[c * 128 : (c + 1) * 128, 128:256] = im.T
        got = jnp.dot(left[0 : (c + 1) * 128, :], right[c % 2], preferred_element_type=jnp.float32)
        for r in range(c + 1):
            t = tile_index(r, c)
            stage[t, 0] = got[r * 128 : (r + 1) * 128, 0:128] * (1.0 / 128)
            stage[t, 1] = got[r * 128 : (r + 1) * 128, 128:256] * (1.0 / 128)
        for r in range(c + 1):
            t = tile_index(r, c)
            pltpu.make_async_copy(stage.at[t], o_ref.at[t], sem).start()
    pltpu.make_async_copy(stage, o_ref, sem).wait()


def correlate(got):
    return pl.pallas_call(
        correlate_kernel,
        out_shape=jax.ShapeDtypeStruct((TILES, 2, TB, TB), jnp.float32),
        in_specs=[pl.BlockSpec(memory_space=pltpu.VMEM)],
        out_specs=pl.BlockSpec(memory_space=pl.ANY),
        scratch_shapes=[
            pltpu.VMEM((BLOCKS * 128, 256), jnp.bfloat16),
            pltpu.VMEM((2, 256, 256), jnp.bfloat16),
            pltpu.VMEM((TILES, 2, TB, TB), jnp.float32),
            pltpu.SemaphoreType.DMA,
        ],
        compiler_params=pltpu.CompilerParams(vmem_limit_bytes=40 << 20),
        name="correlate",
    )(got)


def shards(voltages):
    got = spread(voltages, jnp.asarray(filter_rows()))
    return correlate(got)[None]


def solution(mesh):
    return jax.shard_map(
        shards,
        mesh=mesh,
        in_specs=(P("inp", "spec"),),
        out_specs=P(("inp", "spec"), None, None, None, None),
        check_vma=False,
    )
```

time: 103 us -> 45.9 us (0.45)
  Pallas kernels: 0 us -> 40.1 us
  blocking collectives: 30.4 us -> 0 us
  local copies, waits for them, and re-layouts: 26.6 us -> 5.57 us
  other arithmetic: 18.6 us -> 0 us
  matrix products: 16.1 us -> 0 us
  waiting for transfers between devices: 5.88 us -> 0 us
  starting transfers between devices: 4.57 us -> 0 us
    pallas_call x0 -> x2, Pallas kernels: none -> 40.1 us  [the longest x1 33.7 us: spread(): pl.pallas_call(spread_kernel, out_shape=jax.ShapeDtypeStruct((128, 5, 8,...]
    all_to_all x1 -> x0, blocking collectives: 30.4 us -> none  [one_exchange(): lax.all_to_all(pieces, axis, split_axis=0, concat_axis=0, tiled=True)]
    gather x1 -> x0, local copies, waits for them, and re-layouts: 17.6 us -> none  [correlate_block(): return tiled[:, row_index, col_index]]
    dot_general x3 -> x0, matrix products: 16.1 us -> none  [the longest x1 11.3 us: tap_products(): jnp.einsum('ifn,tnq->tqfi', frames, kernel, preferred_element_type=jnp.fl...]
    transpose x1 -> x0, other arithmetic: 11.7 us -> none  [correlate_block(): pair_parts.reshape(chan_count, 2, row_blocks, TB, row_blocks, TB)]
    ppermute x1 -> x0, waiting for transfers between devices: 5.88 us -> none  [shifted(): lax.ppermute(value, axis, [(source, source + steps) for source in range(i...]
    unnamed x2 -> x4, local copies, waits for them, and re-layouts: 0.01 us -> 5.57 us
    ppermute x1 -> x0, starting transfers between devices: 4.57 us -> none  [shifted(): lax.ppermute(value, axis, [(source, source + steps) for source in range(i...]
  transfers between devices with their start and end apart: 1 -> 0, of which waited for: 1 -> 0; matrix products, arithmetic and copies ran while one was open for 2% -> 0% of each run, Pallas kernels for 0% -> 0%
where the time goes in v1:
time: 45.9 us; the launch traced here: 45.7 us
  Pallas kernels  40.1 us (87%)
  local copies, waits for them, and re-layouts  5.57 us (12%)
    pallas_call x1, Pallas kernels, spread(): pl.pallas_call(spread_kernel, out_shape=jax.ShapeDtypeStruct((128, 5, 8,...  33.7 us
    pallas_call x1, Pallas kernels, correlate(): pl.pallas_call(correlate_kernel, out_shape=jax.ShapeDtypeStruct((TILES, 2...  6.44 us
    unnamed x4, local copies, waits for them, and re-layouts  5.57 us

profile of v1, /device:TPU:1, one launch (start us, length us, event | category | flops | bytes accessed | tf_op | source)
XLA Modules:
  0.0 45.7 jit_solution(7448761124735760671)
XLA Ops:
  0.0 0.0 copy-start
  0.0 3.4 %copy-done = bf16[128,32768]{1,0:T(8,128)(2,1)S(1)} copy-done((bf16[128,32768]{1,0:T(8,128)(2,1)S(1)}, bf16[128,32768]{1,0:T(8,128)(2,1)}, u32[]{:S(2)}) %copy-start) | copy-done | bytes 8388632
  3.4 0.0 copy-start.1
  3.4 2.2 %copy-done.1 = bf16[4,256,2048]{2,1,0:T(8,128)(2,1)S(1)} copy-done((bf16[4,256,2048]{2,1,0:T(8,128)(2,1)S(1)}, bf16[4,256,2048]{2,1,0:T(8,128)(2,1)}, u32[]{:S(2)}) %copy-start.1) | copy-done | bytes 4194328
  5.6 33.7 %spread.1.r_ref = bf16[128,5,8,128]{3,2,1,0:T(8,128)(2,1)S(1)} custom-call(bf16[128,32768]{1,0:T(8,128)(2,1)S(1)} %copy-done, bf16[4,256,2048]{2,1,0:T(8,128)(2,1)S(1)} %copy-done.1), custom_call_target="tpu_custom_call" | custom-call | tf_op jit(solution)/shard_map/spread/pallas_call | solution.py:152
  39.3 6.4 %correlate.1 = f32[136,2,128,128]{3,2,1,0:T(8,128)} custom-call(bf16[128,5,8,128]{3,2,1,0:T(8,128)(2,1)S(1)} %spread.1.r_ref), custom_call_target="tpu_custom_call" | custom-call | tf_op jit(solution)/shard_map/correlate/pallas_call | solution.py:216
Async XLA Ops:
  0.0 3.4 %copy-start = (bf16[128,32768]{1,0:T(8,128)(2,1)S(1)}, bf16[128,32768]{1,0:T(8,128)(2,1)}, u32[]{:S(2)}) copy-start(bf16[128,32768]{1,0:T(8,128)(2,1)} %v_ref.1) | copy-start | bytes 25165828
  3.4 2.2 %copy-start.1 = (bf16[4,256,2048]{2,1,0:T(8,128)(2,1)S(1)}, bf16[4,256,2048]{2,1,0:T(8,128)(2,1)}, u32[]{:S(2)}) copy-start(bf16[4,256,2048]{2,1,0:T(8,128)(2,1)} %constant.2.clone.k_ref) | copy-start | bytes 12582916

commit v2 on v1

v2 whole, which is shorter than its diff:
```python
import math
import random

import jax
import jax.numpy as jnp
from jax import lax
from jax.experimental import pallas as pl
from jax.experimental.pallas import tpu as pltpu
from jax.sharding import PartitionSpec as P

NFFT = 2048
NTAP = 4
TB = 128
CHANS = 128
STEP = 8
FRAMES = 16
HALF = FRAMES // 2
FOLD = 256
TURNS = NFFT // FOLD
GROUP = 32
BATCH = 16
LOGICAL = pl.DeviceIdType.LOGICAL


def far_first():
    offsets = [(k >> 5, (k >> 3) & 3, (k >> 1) & 3, k & 1) for k in range(1, 128)]
    random.Random(1).shuffle(offsets)
    return sorted(offsets, key=lambda o: -sum(min(d, 4 - d) for d in o[:3]))


def signed_windows():
    row = lax.broadcasted_iota(jnp.int32, (2 * TURNS * NTAP, 128), 0)
    lane = lax.broadcasted_iota(jnp.int32, (2 * TURNS * NTAP, 128), 1)
    half, turn, tap = row // (TURNS * NTAP), (row // NTAP) % TURNS, row % NTAP
    pos = (tap * NFFT + turn * FOLD + half * 128 + lane).astype(jnp.float32)
    hann = 0.5 - 0.5 * jnp.cos(pos * (2.0 * math.pi / (NTAP * NFFT)))
    angle = (pos - 0.5 * NTAP * NFFT) * (math.pi / NFFT)
    middle = angle == 0.0
    sinc = jnp.where(middle, 1.0, jnp.sin(angle) / jnp.where(middle, 1.0, angle))
    return sinc * hann * (1 - 2 * (turn % 2)).astype(jnp.float32)


def first_columns():
    q = lax.broadcasted_iota(jnp.int32, (2 * CHANS, FOLD), 0)
    m = lax.broadcasted_iota(jnp.int32, (2 * CHANS, FOLD), 1)
    freq = q // 2 * STEP + STEP // 2
    phase = (m * freq + q % 2 * (NFFT // 4)) % NFFT
    return jnp.cos(phase.astype(jnp.float32) * (2.0 * math.pi / NFFT)) * (1.0 / math.sqrt(NFFT))


def spread_kernel(v_ref, r_ref, vbuf, wide, columns, folded, acc, tail, out, vsem, ssem, rsem, lsem):
    a, b = lax.axis_index("inp"), lax.axis_index("spec")
    me = a * 8 + b
    y, x_lo, core = lax.div(a, 4), lax.rem(lax.div(a, 2), 2), lax.rem(a, 2)
    x, z = lax.div(b, 4) * 2 + x_lo, lax.rem(b, 4)
    not_last = b < 7

    halves = [(0, HALF, 0, HALF), (HALF - NTAP + 1, FRAMES, HALF, FRAMES + NTAP - 1)]

    def v_copy(h, g):
        rows = pl.ds(pl.multiple_of(g * GROUP, GROUP), GROUP)
        lanes = pl.ds(h * HALF * NFFT, HALF * NFFT)
        return pltpu.make_async_copy(v_ref.at[rows, lanes], vbuf.at[rows, lanes], vsem.at[h, g])

    for h in range(2):
        for g in range(128 // GROUP):
            v_copy(h, g).start()

    barrier = pltpu.get_barrier_semaphore()

    def greet(k, carry):
        pl.semaphore_signal(barrier, inc=1, device_id=lax.rem(me + k, 128), device_id_type=LOGICAL)
        return carry

    lax.fori_loop(1, 128, greet, 0)
    tail[...] = jnp.zeros_like(tail)
    windows = signed_windows()
    for k in range(2 * TURNS * NTAP):
        wide[k] = jnp.broadcast_to(windows[k : k + 1, :], (8, 128))
    exact = first_columns()
    high = exact.astype(jnp.bfloat16)
    columns[:, 0:FOLD] = high
    columns[:, FOLD : 2 * FOLD] = high
    columns[:, 2 * FOLD :] = (exact - high.astype(jnp.float32)).astype(jnp.bfloat16)

    def fold(h, i):
        g, part = lax.div(i, 2), lax.rem(i, 2)
        f_begin, f_end, s_begin, s_end = halves[h]

        @pl.when(part == 0)
        def _():
            v_copy(h, g).wait()

        rows = pl.ds(pl.multiple_of(g * GROUP, GROUP), GROUP)
        sums = {}
        for f in range(f_begin, f_end):
            for u in range(TURNS):
                lanes = pl.ds(pl.multiple_of(f * NFFT + u * FOLD + part * 128, 128), 128)
                v = vbuf[rows, lanes].astype(jnp.float32).reshape(GROUP // 8, 8, 128)
                for t in range(NTAP):
                    s = f - t + NTAP - 1
                    if s_begin <= s < s_end:
                        term = v * wide[part * (TURNS * NTAP) + u * NTAP + t]
                        sums[s] = sums[s] + term if s in sums else term
            for s in [s for s in sums if s <= f or f == f_end - 1]:
                whole = sums.pop(s).reshape(GROUP, 128)
                high = whole.astype(jnp.bfloat16)
                low = (whole - high.astype(jnp.float32)).astype(jnp.bfloat16)
                folded[s - s_begin, rows, pl.ds(pl.multiple_of(part * 128, 128), 128)] = high
                folded[s - s_begin, rows, pl.ds(pl.multiple_of(part * 128 + FOLD, 128), 128)] = low

    def spectrum(n, count):
        frames = folded[pl.ds(n, count)].reshape(count * 128, 2 * FOLD)
        dims = (((1,), (1,)), ((), ()))
        got = lax.dot_general(columns[:, : 2 * FOLD], frames, dims, preferred_element_type=jnp.float32)
        got = got + lax.dot_general(columns[:, 2 * FOLD :], frames[:, :FOLD], dims, preferred_element_type=jnp.float32)
        return [got[:, k * 128 : (k + 1) * 128] for k in range(count)]

    def send(to, slabs, k):
        pltpu.make_async_remote_copy(
            src_ref=out.at[to, slabs],
            dst_ref=r_ref.at[me, slabs],
            send_sem=ssem.at[k],
            recv_sem=rsem.at[k],
            device_id=to,
            device_id_type=LOGICAL,
        ).start()

    parts = [pl.ds(0, 2), pl.ds(3, 2), pl.ds(2, 1)]

    def pack(to, h):
        for part in range(2):
            rows = pl.ds(pl.multiple_of((2 * to + part) * HALF, HALF), HALF)
            out[to, 3 * h + part] = acc[rows, :].astype(jnp.bfloat16)
        if h == 1:
            out[to, 2] = tail[pl.ds(pl.multiple_of(to * 8, 8), 8), :].astype(jnp.bfloat16)

    targets = []
    for dx, dy, dz, dc in far_first():
        x_to, y_to, z_to = lax.rem(x + dx, 4), lax.rem(y + dy, 4), lax.rem(z + dz, 4)
        targets.append(y_to * 32 + (lax.rem(x_to, 2) * 2 + lax.rem(core + dc, 2)) * 8 + lax.div(x_to, 2) * 4 + z_to)

    for h in range(2):

        def fold_step(i, carry):
            fold(h, i)
            return carry

        lax.fori_loop(0, 2 * (128 // GROUP), fold_step, 0)

        def main(n, carry):
            for k, got in enumerate(spectrum(2 * n, 2)):
                for g in range(2 * CHANS // 8):
                    acc[pl.ds(8 * g * HALF + 2 * n + k, 8, stride=HALF), :] = got[8 * g : 8 * g + 8]
            return carry

        lax.fori_loop(0, HALF // 2, main, 0)
        if h == 0:
            pl.semaphore_wait(barrier, 127)
        else:
            for k, got in enumerate(spectrum(HALF, NTAP - 1)):
                for g in range(2 * CHANS // 8):
                    tail[pl.ds(8 * g * 4 + k, 8, stride=4), :] = got[8 * g : 8 * g + 8]

        for n in range(0, 127, BATCH):
            batch = targets[n : n + BATCH]
            for to in batch:
                pack(to, h)
            for to in batch:
                send(to, parts[h], h)
            if h == 1:

                @pl.when(not_last)
                def _(batch=batch):
                    for to in batch:
                        send(to, parts[2], 2)

        pack(me, h)

    own = pltpu.make_async_copy(out.at[me], r_ref.at[me], lsem)
    own.start()
    own.wait()

    def landed(count, k, sem):
        block = r_ref.at[pl.ds(0, count), parts[k]]
        pltpu.make_async_copy(block, block, sem.at[k]).wait()

    for k in range(2):
        landed(127, k, ssem)
        landed(127, k, rsem)

    @pl.when(not_last)
    def _():
        landed(127, 2, ssem)
        landed(111, 2, rsem)

    @pl.when(jnp.logical_not(not_last))
    def _():
        landed(112, 2, rsem)


def spread(v):
    return pl.pallas_call(
        spread_kernel,
        out_shape=jax.ShapeDtypeStruct((128, 5, 8, 128), jnp.bfloat16),
        in_specs=[pl.BlockSpec(memory_space=pl.ANY)],
        out_specs=pl.BlockSpec(memory_space=pltpu.VMEM),
        scratch_shapes=[
            pltpu.VMEM((128, FRAMES * NFFT), jnp.bfloat16),
            pltpu.VMEM((2 * TURNS * NTAP, 8, 128), jnp.float32),
            pltpu.VMEM((2 * CHANS, 3 * FOLD), jnp.bfloat16),
            pltpu.VMEM((HALF + NTAP - 1, 128, 2 * FOLD), jnp.bfloat16),
            pltpu.VMEM((2 * CHANS * HALF, 128), jnp.float32),
            pltpu.VMEM((2 * CHANS * 4, 128), jnp.float32),
            pltpu.VMEM((CHANS, 5, 8, 128), jnp.bfloat16),
            pltpu.SemaphoreType.DMA((2, 128 // GROUP)),
            pltpu.SemaphoreType.DMA((3,)),
            pltpu.SemaphoreType.DMA((3,)),
            pltpu.SemaphoreType.DMA,
        ],
        compiler_params=pltpu.CompilerParams(collective_id=0, has_side_effects=True, vmem_limit_bytes=52 << 20),
        name="spread",
    )(v)


BLOCKS = 16
TILES = BLOCKS * (BLOCKS + 1) // 2


def tile_index(r, c):
    return r * BLOCKS - r * (r - 1) // 2 + (c - r)


def correlate_kernel(r_ref, o_ref, left, right, stage, sem):
    row = lax.broadcasted_iota(jnp.int32, (8, 128), 0)
    for c in range(BLOCKS):
        for part in range(2):
            for b in range(8):
                src = c * 8 + b
                head = r_ref[src, part].astype(jnp.float32)
                rest = r_ref[src, 3 + part].astype(jnp.float32)
                if b > 0:
                    terms = r_ref[src - 1, 2].astype(jnp.float32)
                    if part == 1:
                        terms = jnp.concatenate([terms[4:], terms[:4]], axis=0)
                    head = head + jnp.where(row < NTAP - 1, terms, 0.0)
                both = jnp.concatenate([head, rest], axis=0)
                at = part * 128 + b * 16
                right[c % 2, pl.ds(at, 16), 0:128] = both.astype(jnp.bfloat16)
        re, im = right[c % 2, 0:128, 0:128], right[c % 2, 128:256, 0:128]
        right[c % 2, 0:128, 128:256] = -im
        right[c % 2, 128:256, 128:256] = re
        left[c * 128 : (c + 1) * 128, 0:128] = re.T
        left[c * 128 : (c + 1) * 128, 128:256] = im.T
        got = jnp.dot(left[0 : (c + 1) * 128, :], right[c % 2], preferred_element_type=jnp.float32)
        for r in range(c + 1):
            t = tile_index(r, c)
            stage[t, 0] = got[r * 128 : (r + 1) * 128, 0:128] * (1.0 / 128)
            stage[t, 1] = got[r * 128 : (r + 1) * 128, 128:256] * (1.0 / 128)
        for r in range(c + 1):
            t = tile_index(r, c)
            pltpu.make_async_copy(stage.at[t], o_ref.at[t], sem).start()
    pltpu.make_async_copy(stage, o_ref, sem).wait()


def correlate(got):
    return pl.pallas_call(
        correlate_kernel,
        out_shape=jax.ShapeDtypeStruct((TILES, 2, TB, TB), jnp.float32),
        in_specs=[pl.BlockSpec(memory_space=pltpu.VMEM)],
        out_specs=pl.BlockSpec(memory_space=pl.ANY),
        scratch_shapes=[
            pltpu.VMEM((BLOCKS * 128, 256), jnp.bfloat16),
            pltpu.VMEM((2, 256, 256), jnp.bfloat16),
            pltpu.VMEM((TILES, 2, TB, TB), jnp.float32),
            pltpu.SemaphoreType.DMA,
        ],
        compiler_params=pltpu.CompilerParams(vmem_limit_bytes=40 << 20),
        name="correlate",
    )(got)


def shards(voltages):
    got = spread(voltages)
    return correlate(got)[None]


def solution(mesh):
    return jax.shard_map(
        shards,
        mesh=mesh,
        in_specs=(P("inp", "spec"),),
        out_specs=P(("inp", "spec"), None, None, None, None),
        check_vma=False,
    )
```

time: 45.9 us -> 36.2 us (0.79)
  local copies, waits for them, and re-layouts: 5.57 us -> 0 us
  Pallas kernels: 40.1 us -> 36.1 us
    unnamed x4 -> x0, local copies, waits for them, and re-layouts: 5.57 us -> none
    pallas_call x1, Pallas kernels: 33.7 us -> 29.7 us  [spread(): pl.pallas_call(spread_kernel, out_shape=jax.ShapeDtypeStruct((128, 5, 8,...]
where the time goes in v2:
time: 36.2 us; the launch traced here: 36.1 us
  Pallas kernels  36.1 us (100%)
    pallas_call x1, Pallas kernels, spread(): pl.pallas_call(spread_kernel, out_shape=jax.ShapeDtypeStruct((128, 5, 8,...  29.7 us
    pallas_call x1, Pallas kernels, correlate(): pl.pallas_call(correlate_kernel, out_shape=jax.ShapeDtypeStruct((TILES, 2...  6.44 us

profile of v2, /device:TPU:1, one launch (start us, length us, event | category | flops | bytes accessed | tf_op | source)
XLA Modules:
  0.0 36.1 jit_solution(2042624253020297292)
XLA Ops:
  0.0 29.7 %spread.1.r_ref = bf16[128,5,8,128]{3,2,1,0:T(8,128)(2,1)S(1)} custom-call(bf16[128,32768]{1,0:T(8,128)(2,1)} %v_ref.1), custom_call_target="tpu_custom_call" | custom-call | tf_op jit(solution)/shard_map/spread/pallas_call | solution.py:203
  29.7 6.4 %correlate.1 = f32[136,2,128,128]{3,2,1,0:T(8,128)} custom-call(bf16[128,5,8,128]{3,2,1,0:T(8,128)(2,1)S(1)} %spread.1.r_ref), custom_call_target="tpu_custom_call" | custom-call | tf_op jit(solution)/shard_map/correlate/pallas_call | solution.py:267

commit v3 on v2

--- a/solution.py
+++ b/solution.py
@@ -55,7 +55,7 @@
     x, z = lax.div(b, 4) * 2 + x_lo, lax.rem(b, 4)
     not_last = b < 7
 
-    halves = [(0, HALF, 0, HALF), (HALF - NTAP + 1, FRAMES, HALF, FRAMES + NTAP - 1)]
+    stages = [(0, HALF, 0, HALF), (HALF - NTAP + 1, FRAMES, HALF, FRAMES), (FRAMES - NTAP + 1, FRAMES, FRAMES, FRAMES + NTAP - 1)]
 
     def v_copy(h, g):
         rows = pl.ds(pl.multiple_of(g * GROUP, GROUP), GROUP)
@@ -85,11 +85,13 @@
 
     def fold(h, i):
         g, part = lax.div(i, 2), lax.rem(i, 2)
-        f_begin, f_end, s_begin, s_end = halves[h]
-
-        @pl.when(part == 0)
-        def _():
-            v_copy(h, g).wait()
+        f_begin, f_end, s_begin, s_end = stages[h]
+
+        if h < 2:
+
+            @pl.when(part == 0)
+            def _():
+                v_copy(h, g).wait()
 
         rows = pl.ds(pl.multiple_of(g * GROUP, GROUP), GROUP)
         sums = {}
@@ -129,53 +131,49 @@
     parts = [pl.ds(0, 2), pl.ds(3, 2), pl.ds(2, 1)]
 
     def pack(to, h):
+        if h == 2:
+            out[to, 2] = tail[pl.ds(pl.multiple_of(to * 8, 8), 8), :].astype(jnp.bfloat16)
+            return
         for part in range(2):
             rows = pl.ds(pl.multiple_of((2 * to + part) * HALF, HALF), HALF)
             out[to, 3 * h + part] = acc[rows, :].astype(jnp.bfloat16)
-        if h == 1:
-            out[to, 2] = tail[pl.ds(pl.multiple_of(to * 8, 8), 8), :].astype(jnp.bfloat16)
-
-    targets = []
-    for dx, dy, dz, dc in far_first():
-        x_to, y_to, z_to = lax.rem(x + dx, 4), lax.rem(y + dy, 4), lax.rem(z + dz, 4)
-        targets.append(y_to * 32 + (lax.rem(x_to, 2) * 2 + lax.rem(core + dc, 2)) * 8 + lax.div(x_to, 2) * 4 + z_to)
-
-    for h in range(2):
-
-        def fold_step(i, carry):
-            fold(h, i)
-            return carry
-
-        lax.fori_loop(0, 2 * (128 // GROUP), fold_step, 0)
-
-        def main(n, carry):
-            for k, got in enumerate(spectrum(2 * n, 2)):
-                for g in range(2 * CHANS // 8):
-                    acc[pl.ds(8 * g * HALF + 2 * n + k, 8, stride=HALF), :] = got[8 * g : 8 * g + 8]
-            return carry
-
-        lax.fori_loop(0, HALF // 2, main, 0)
-        if h == 0:
-            pl.semaphore_wait(barrier, 127)
-        else:
-            for k, got in enumerate(spectrum(HALF, NTAP - 1)):
-                for g in range(2 * CHANS // 8):
-                    tail[pl.ds(8 * g * 4 + k, 8, stride=4), :] = got[8 * g : 8 * g + 8]
-
+
+    def deliver(h):
         for n in range(0, 127, BATCH):
             batch = targets[n : n + BATCH]
             for to in batch:
                 pack(to, h)
             for to in batch:
                 send(to, parts[h], h)
-            if h == 1:
-
-                @pl.when(not_last)
-                def _(batch=batch):
-                    for to in batch:
-                        send(to, parts[2], 2)
-
         pack(me, h)
+
+    targets = []
+    for dx, dy, dz, dc in far_first():
+        x_to, y_to, z_to = lax.rem(x + dx, 4), lax.rem(y + dy, 4), lax.rem(z + dz, 4)
+        targets.append(y_to * 32 + (lax.rem(x_to, 2) * 2 + lax.rem(core + dc, 2)) * 8 + lax.div(x_to, 2) * 4 + z_to)
+
+    def stage(h):
+        def fold_step(i, carry):
+            fold(h, i)
+            return carry
+
+        lax.fori_loop(0, 2 * (128 // GROUP), fold_step, 0)
+        if h < 2:
+            for n in range(0, HALF, 2):
+                for k, got in enumerate(spectrum(n, 2)):
+                    for g in range(2 * CHANS // 8):
+                        acc[pl.ds(8 * g * HALF + n + k, 8, stride=HALF), :] = got[8 * g : 8 * g + 8]
+        else:
+            for k, got in enumerate(spectrum(0, NTAP - 1)):
+                for g in range(2 * CHANS // 8):
+                    tail[pl.ds(8 * g * 4 + k, 8, stride=4), :] = got[8 * g : 8 * g + 8]
+        if h == 0:
+            pl.semaphore_wait(barrier, 127)
+        deliver(h)
+
+    stage(0)
+    stage(1)
+    pl.when(not_last)(lambda: stage(2))
 
     own = pltpu.make_async_copy(out.at[me], r_ref.at[me], lsem)
     own.start()
@@ -209,7 +207,7 @@
             pltpu.VMEM((128, FRAMES * NFFT), jnp.bfloat16),
             pltpu.VMEM((2 * TURNS * NTAP, 8, 128), jnp.float32),
             pltpu.VMEM((2 * CHANS, 3 * FOLD), jnp.bfloat16),
-            pltpu.VMEM((HALF + NTAP - 1, 128, 2 * FOLD), jnp.bfloat16),
+            pltpu.VMEM((HALF, 128, 2 * FOLD), jnp.bfloat16),
             pltpu.VMEM((2 * CHANS * HALF, 128), jnp.float32),
             pltpu.VMEM((2 * CHANS * 4, 128), jnp.float32),
             pltpu.VMEM((CHANS, 5, 8, 128), jnp.bfloat16),

time: 36.2 us -> 36 us (level)
  no operation moved by 1% of the time
where the time goes in v3:
time: 36 us; the launch traced here: 35.9 us
  Pallas kernels  35.9 us (100%)
    pallas_call x1, Pallas kernels, spread(): pl.pallas_call(spread_kernel, out_shape=jax.ShapeDtypeStruct((128, 5, 8,...  29.5 us
    pallas_call x1, Pallas kernels, correlate(): pl.pallas_call(correlate_kernel, out_shape=jax.ShapeDtypeStruct((TILES, 2...  6.44 us

profile of v3, /device:TPU:1, one launch (start us, length us, event | category | flops | bytes accessed | tf_op | source)
XLA Modules:
  0.0 35.9 jit_solution(12194653120439258775)
XLA Ops:
  0.0 29.5 %spread.1.r_ref = bf16[128,5,8,128]{3,2,1,0:T(8,128)(2,1)S(1)} custom-call(bf16[128,32768]{1,0:T(8,128)(2,1)} %v_ref.1), custom_call_target="tpu_custom_call" | custom-call | tf_op jit(solution)/shard_map/spread/pallas_call | solution.py:201
  29.5 6.4 %correlate.1 = f32[136,2,128,128]{3,2,1,0:T(8,128)} custom-call(bf16[128,5,8,128]{3,2,1,0:T(8,128)(2,1)S(1)} %spread.1.r_ref), custom_call_target="tpu_custom_call" | custom-call | tf_op jit(solution)/shard_map/correlate/pallas_call | solution.py:265

commit v4 on v3

--- a/solution.py
+++ b/solution.py
@@ -1,3 +1,4 @@
+import functools
 import math
 import random
 
@@ -19,13 +20,15 @@
 TURNS = NFFT // FOLD
 GROUP = 32
 BATCH = 16
+Z_LEAD, Y_LEAD, X_LEAD = 0.5, 0.2, 0.1
 LOGICAL = pl.DeviceIdType.LOGICAL
 
 
-def far_first():
-    offsets = [(k >> 5, (k >> 3) & 3, (k >> 1) & 3, k & 1) for k in range(1, 128)]
-    random.Random(1).shuffle(offsets)
-    return sorted(offsets, key=lambda o: -sum(min(d, 4 - d) for d in o[:3]))
+def order():
+    places = [(k >> 5, (k >> 3) & 3, (k >> 1) & 3, k & 1) for k in range(128)]
+    draw = random.Random(1)
+    key = {o: draw.random() + Z_LEAD * o[2] / 3 + Y_LEAD * o[1] / 3 - X_LEAD * min(o[0], 4 - o[0]) for o in places}
+    return sorted(places, key=key.get)
 
 
 def signed_windows():
@@ -72,7 +75,7 @@
         pl.semaphore_signal(barrier, inc=1, device_id=lax.rem(me + k, 128), device_id_type=LOGICAL)
         return carry
 
-    lax.fori_loop(1, 128, greet, 0)
+    lax.fori_loop(1, 128, greet, 0, unroll=127)
     tail[...] = jnp.zeros_like(tail)
     windows = signed_windows()
     for k in range(2 * TURNS * NTAP):
@@ -136,21 +139,33 @@
             return
         for part in range(2):
             rows = pl.ds(pl.multiple_of((2 * to + part) * HALF, HALF), HALF)
-            out[to, 3 * h + part] = acc[rows, :].astype(jnp.bfloat16)
-
-    def deliver(h):
-        for n in range(0, 127, BATCH):
+            out[to, 3 * h + part] = acc[h, rows, :].astype(jnp.bfloat16)
+
+    def deliver(*which):
+        for n in range(0, 128, BATCH):
             batch = targets[n : n + BATCH]
-            for to in batch:
-                pack(to, h)
-            for to in batch:
-                send(to, parts[h], h)
-        pack(me, h)
+            for to, _ in batch:
+                for h in which:
+                    pack(to, h)
+            for h in which:
+
+                def go(batch=batch, h=h):
+                    for to, maybe_own in batch:
+                        if maybe_own:
+                            pl.when(to != me)(functools.partial(send, to, parts[h], h))
+                        else:
+                            send(to, parts[h], h)
+
+                if h == 2:
+                    pl.when(not_last)(go)
+                else:
+                    go()
 
     targets = []
-    for dx, dy, dz, dc in far_first():
-        x_to, y_to, z_to = lax.rem(x + dx, 4), lax.rem(y + dy, 4), lax.rem(z + dz, 4)
-        targets.append(y_to * 32 + (lax.rem(x_to, 2) * 2 + lax.rem(core + dc, 2)) * 8 + lax.div(x_to, 2) * 4 + z_to)
+    for dx, y_to, z_to, dc in order():
+        x_to = lax.rem(x + dx, 4)
+        to = y_to * 32 + (lax.rem(x_to, 2) * 2 + lax.rem(core + dc, 2)) * 8 + lax.div(x_to, 2) * 4 + z_to
+        targets.append((to, dx == 0 and dc == 0))
 
     def stage(h):
         def fold_step(i, carry):
@@ -162,18 +177,18 @@
             for n in range(0, HALF, 2):
                 for k, got in enumerate(spectrum(n, 2)):
                     for g in range(2 * CHANS // 8):
-                        acc[pl.ds(8 * g * HALF + n + k, 8, stride=HALF), :] = got[8 * g : 8 * g + 8]
+                        acc[h, pl.ds(8 * g * HALF + n + k, 8, stride=HALF), :] = got[8 * g : 8 * g + 8]
         else:
             for k, got in enumerate(spectrum(0, NTAP - 1)):
                 for g in range(2 * CHANS // 8):
                     tail[pl.ds(8 * g * 4 + k, 8, stride=4), :] = got[8 * g : 8 * g + 8]
-        if h == 0:
-            pl.semaphore_wait(barrier, 127)
-        deliver(h)
 
     stage(0)
+    pl.semaphore_wait(barrier, 127)
+    deliver(0)
     stage(1)
     pl.when(not_last)(lambda: stage(2))
+    deliver(1, 2)
 
     own = pltpu.make_async_copy(out.at[me], r_ref.at[me], lsem)
     own.start()
@@ -208,7 +223,7 @@
             pltpu.VMEM((2 * TURNS * NTAP, 8, 128), jnp.float32),
             pltpu.VMEM((2 * CHANS, 3 * FOLD), jnp.bfloat16),
             pltpu.VMEM((HALF, 128, 2 * FOLD), jnp.bfloat16),
-            pltpu.VMEM((2 * CHANS * HALF, 128), jnp.float32),
+            pltpu.VMEM((2, 2 * CHANS * HALF, 128), jnp.float32),
             pltpu.VMEM((2 * CHANS * 4, 128), jnp.float32),
             pltpu.VMEM((CHANS, 5, 8, 128), jnp.bfloat16),
             pltpu.SemaphoreType.DMA((2, 128 // GROUP)),
@@ -257,7 +272,8 @@
             stage[t, 1] = got[r * 128 : (r + 1) * 128, 128:256] * (1.0 / 128)
         for r in range(c + 1):
             t = tile_index(r, c)
-            pltpu.make_async_copy(stage.at[t], o_ref.at[t], sem).start()
+            for part in range(2):
+                pltpu.make_async_copy(stage.at[t, part], o_ref.at[t, part], sem).start()
     pltpu.make_async_copy(stage, o_ref, sem).wait()
 
 

time: 36 us -> 34.8 us (0.967)
  Pallas kernels: 35.9 us -> 34.7 us
    pallas_call x1, Pallas kernels: 29.5 us -> 28.3 us  [spread(): pl.pallas_call(spread_kernel, out_shape=jax.ShapeDtypeStruct((128, 5, 8,...]
where the time goes in v4:
time: 34.8 us; the launch traced here: 34.7 us
  Pallas kernels  34.7 us (100%)
    pallas_call x1, Pallas kernels, spread(): pl.pallas_call(spread_kernel, out_shape=jax.ShapeDtypeStruct((128, 5, 8,...  28.3 us
    pallas_call x1, Pallas kernels, correlate(): pl.pallas_call(correlate_kernel, out_shape=jax.ShapeDtypeStruct((TILES, 2...  6.42 us

profile of v4, /device:TPU:1, one launch (start us, length us, event | category | flops | bytes accessed | tf_op | source)
XLA Modules:
  0.0 34.7 jit_solution(7885648513461666842)
XLA Ops:
  0.0 28.3 %spread.1.r_ref = bf16[128,5,8,128]{3,2,1,0:T(8,128)(2,1)S(1)} custom-call(bf16[128,32768]{1,0:T(8,128)(2,1)} %v_ref.1), custom_call_target="tpu_custom_call" | custom-call | tf_op jit(solution)/shard_map/spread/pallas_call | solution.py:216
  28.3 6.4 %correlate.1 = f32[136,2,128,128]{3,2,1,0:T(8,128)} custom-call(bf16[128,5,8,128]{3,2,1,0:T(8,128)(2,1)S(1)} %spread.1.r_ref), custom_call_target="tpu_custom_call" | custom-call | tf_op jit(solution)/shard_map/correlate/pallas_call | solution.py:281

commit v5 on v4

--- a/solution.py
+++ b/solution.py
@@ -19,7 +19,7 @@
 FOLD = 256
 TURNS = NFFT // FOLD
 GROUP = 32
-BATCH = 16
+BATCH = 8
 Z_LEAD, Y_LEAD, X_LEAD = 0.5, 0.2, 0.1
 LOGICAL = pl.DeviceIdType.LOGICAL
 

time: 34.8 us -> 34 us (0.977)
  Pallas kernels: 34.7 us -> 33.7 us
    pallas_call x1, Pallas kernels: 28.3 us -> 27.3 us  [spread(): pl.pallas_call(spread_kernel, out_shape=jax.ShapeDtypeStruct((128, 5, 8,...]
where the time goes in v5:
time: 34 us; the launch traced here: 33.7 us
  Pallas kernels  33.7 us (99%)
    pallas_call x1, Pallas kernels, spread(): pl.pallas_call(spread_kernel, out_shape=jax.ShapeDtypeStruct((128, 5, 8,...  27.3 us
    pallas_call x1, Pallas kernels, correlate(): pl.pallas_call(correlate_kernel, out_shape=jax.ShapeDtypeStruct((TILES, 2...  6.42 us

profile of v5, /device:TPU:1, one launch (start us, length us, event | category | flops | bytes accessed | tf_op | source)
XLA Modules:
  0.0 33.7 jit_solution(9952145800611538649)
XLA Ops:
  0.0 27.3 %spread.1.r_ref = bf16[128,5,8,128]{3,2,1,0:T(8,128)(2,1)S(1)} custom-call(bf16[128,32768]{1,0:T(8,128)(2,1)} %v_ref.1), custom_call_target="tpu_custom_call" | custom-call | tf_op jit(solution)/shard_map/spread/pallas_call | solution.py:216
  27.3 6.4 %correlate.1 = f32[136,2,128,128]{3,2,1,0:T(8,128)} custom-call(bf16[128,5,8,128]{3,2,1,0:T(8,128)(2,1)S(1)} %spread.1.r_ref), custom_call_target="tpu_custom_call" | custom-call | tf_op jit(solution)/shard_map/correlate/pallas_call | solution.py:281
